TPU v7x, 32 devices: a whole 2x2x4 slice. The times are simulated.
32 devices in a mesh: shot: 8 (over z, x), sub: 4 (over y, core).
Axes of the slice: x: 2, y: 2, z: 4, core: 2. Of those that a mesh axis runs over, the one named last changes fastest.
Arguments:
- courant: float32 [8, 128, 128, 128], P('shot', 'sub'), may hold values from 0.04 to 0.2
- adjoint_prev: float32 [8, 128, 128, 128], P('shot', 'sub'), may hold values from -6 to 6
- adjoint_now: float32 [8, 128, 128, 128], P('shot', 'sub'), may hold values from -6 to 6
- forward_accel: float32 [8, 4, 128, 128, 128], P('shot', None, 'sub'), may hold values from -6 to 6
- traces: float32 [8, 4, 512], P('shot'), may hold values from -24 to 24
- receivers: int32 [8, 512], P('shot'), may hold values from 0 to 2097151
- owners: int32 [8, 4, 16, 1], P('shot', 'sub'), may hold values from 0 to 7; in each aligned block of 16 rows (0 to 15, 16 to 31, ..., all dimensions but the last counted through in order) at most 2 rows name the same one
- tile_slot: int32 [8, 4, 16], P('shot', 'sub'), may hold values from 0 to 7
Outputs:
- smoothed: float32 [64, 128, 8, 128], P('shot', 'sub')
- adjoint_last: float32 [8, 128, 128, 128], P('shot', 'sub')
Inputs may be any that keep to these rules, and one draw needn't show every extreme that they name: `owners`: among the 16 blocks of one device at most 2 name the same owner, and in some device's blocks one owner is named by exactly 2.
All inputs are finite; a program needn't handle non-finite values.
Results may differ from a plain program's by a relative error of at most 0.00013.
Values sent between devices are 32-bit elements; how exact they have to be, the bound alone decides.
A program may use at most 128 MiB of HBM per device.

v0:
```python
import functools

import jax
import jax.numpy as jnp
from jax import lax
from jax.experimental import pallas as pl
from jax.experimental.pallas import tpu as pltpu
from jax.sharding import PartitionSpec as P

TX = 8
TILES_OWN = 8
CAP = 2
HALO = 4
PAD = 8
MESH = pl.DeviceIdType.MESH

stencil_weights = (-205.0 / 72.0, 8.0 / 5.0, -1.0 / 5.0, 8.0 / 315.0, -1.0 / 560.0)


def prepare_kernel(slab_cells, cols_y, rec_ref, tr_ref, own_ref, slot_ref, src_ref, inv_ref, ids_ref, count_ref):
    steps = src_ref.shape[0]
    zrows = 256

    def zero(i, _):
        src_ref[:, pl.ds(pl.multiple_of(i * zrows, zrows), zrows), :] = jnp.zeros(
            (steps, zrows, cols_y), jnp.float32
        )
        return 0

    lax.fori_loop(0, src_ref.shape[1] // zrows, zero, 0)
    base = lax.axis_index("sub") * slab_cells
    lane = lax.broadcasted_iota(jnp.int32, (1, cols_y), 1)

    def add(r, _):
        off = rec_ref[0, r] - base

        @pl.when((off >= 0) & (off < slab_cells))
        def _():
            row = lax.div(off, cols_y)
            hit = lane == lax.rem(off, cols_y)
            for t in range(steps):
                src_ref[t, pl.ds(row, 1), :] += jnp.where(hit, tr_ref[0, t, r], 0.0)

        return 0

    lax.fori_loop(0, rec_ref.shape[1], add, 0, unroll=4)

    ids_ref[...] = jnp.full(ids_ref.shape, -1, jnp.int32)
    for i in range(count_ref.shape[0]):
        count_ref[i] = 0
    for i in range(inv_ref.shape[0]):
        inv_ref[i] = 0
    for k in range(slot_ref.shape[2]):
        owner = own_ref[0, 0, k, 0]
        place = owner * CAP + count_ref[owner]
        count_ref[owner] = count_ref[owner] + 1
        inv_ref[place] = k
        ids_ref[pl.ds(place, 1)] = jnp.full((1,) + ids_ref.shape[1:], slot_ref[0, 0, k], jnp.int32)


def wave_kernel(
    n_sub, inv_ref, cour_hbm, prev_hbm, now_hbm, acc_hbm, src_hbm,
    last_hbm, send_hbm,
    even, odd, cour, acc, src, grad, packed,
    lsem, tsem, hsend, hrecv, psem, osem,
):
    buf = (even, odd)
    me = lax.axis_index("sub")
    steps, depth, rows, cols = acc.shape
    lo, hi = HALO, HALO + depth
    inner = pl.ds(PAD, rows)

    local = [
        pltpu.make_async_copy(now_hbm.at[0], even.at[lo:hi, inner, :], lsem.at[0]),
        pltpu.make_async_copy(prev_hbm.at[0], odd.at[lo:hi, inner, :], lsem.at[1]),
        pltpu.make_async_copy(cour_hbm.at[0], cour, lsem.at[2]),
    ]
    per_step = [
        (
            pltpu.make_async_copy(src_hbm.at[t], src.at[t], tsem.at[t, 0]),
            pltpu.make_async_copy(acc_hbm.at[0, t], acc.at[t], tsem.at[t, 1]),
        )
        for t in range(steps)
    ]
    for c in local:
        c.start()
    for t in range(steps):
        for c in per_step[t]:
            c.start()

    for ref in buf:
        ref[:, 0:PAD, :] = jnp.zeros((depth + 2 * HALO, PAD, cols), jnp.float32)
        ref[:, PAD + rows :, :] = jnp.zeros((depth + 2 * HALO, PAD, cols), jnp.float32)
        ref[0:lo, inner, :] = jnp.zeros((HALO, rows, cols), jnp.float32)
        ref[hi:, inner, :] = jnp.zeros((HALO, rows, cols), jnp.float32)

    has_up, has_down = me > 0, me < n_sub - 1
    barrier = pltpu.get_barrier_semaphore()

    @pl.when(has_up)
    def _():
        pl.semaphore_signal(barrier, inc=1, device_id={"sub": me - 1}, device_id_type=MESH)

    @pl.when(has_down)
    def _():
        pl.semaphore_signal(barrier, inc=1, device_id={"sub": me + 1}, device_id_type=MESH)

    pl.semaphore_wait(barrier, jnp.minimum(me, 1) + jnp.minimum(n_sub - 1 - me, 1))

    def halos(t):
        b = t % 2
        if t == 0:
            first, final = now_hbm.at[0, 0:HALO], now_hbm.at[0, depth - HALO : depth]
        else:
            first = buf[b].at[lo : lo + HALO, inner, :]
            final = buf[b].at[hi - HALO : hi, inner, :]
        up = pltpu.make_async_remote_copy(
            src_ref=first, dst_ref=buf[b].at[hi : hi + HALO, inner, :],
            send_sem=hsend.at[t, 0], recv_sem=hrecv.at[t, 0],
            device_id={"sub": me - 1}, device_id_type=MESH,
        )
        down = pltpu.make_async_remote_copy(
            src_ref=final, dst_ref=buf[b].at[0:HALO, inner, :],
            send_sem=hsend.at[t, 1], recv_sem=hrecv.at[t, 1],
            device_id={"sub": me + 1}, device_id_type=MESH,
        )
        return up, down

    def start_halos(t):
        up, down = halos(t)

        @pl.when(has_up)
        def _():
            up.start()

        @pl.when(has_down)
        def _():
            down.start()

    def wait_halos(t):
        up, down = halos(t)

        @pl.when(has_up)
        def _():
            up.wait_send()
            down.wait_recv()

        @pl.when(has_down)
        def _():
            down.wait_send()
            up.wait_recv()

    start_halos(0)

    lane = lax.broadcasted_iota(jnp.int32, (TX, cols), 1)
    from_left = [None] + [jnp.where(lane >= d, stencil_weights[d], 0.0) for d in range(1, 5)]
    from_right = [None] + [jnp.where(lane < cols - d, stencil_weights[d], 0.0) for d in range(1, 5)]

    def advance(t, chunks):
        cur, nxt = buf[t % 2], buf[(t + 1) % 2]

        def block(xb, _):
            x0 = pl.multiple_of(xb * TX, TX)
            own = pl.ds(x0, TX)
            here = pl.ds(pl.multiple_of(x0 + PAD, TX), TX)
            for za, zb in chunks:
                col = {z: cur[z + HALO, here, :] for z in range(za - 4, zb + 4)}
                done = []
                for z in range(za, zb):
                    c = col[z]
                    lap = (3.0 * stencil_weights[0]) * c
                    for d in range(1, 5):
                        pair = (col[z + d] + col[z - d]) + (
                            cur[z + HALO, pl.ds(x0 + (PAD + d), TX), :]
                            + cur[z + HALO, pl.ds(x0 + (PAD - d), TX), :]
                        )
                        lap = lap + stencil_weights[d] * pair
                        lap = lap + from_left[d] * pltpu.roll(c, d, 1)
                        lap = lap + from_right[d] * pltpu.roll(c, cols - d, 1)
                    adv = (2.0 * c - nxt[z + HALO, here, :]) + (
                        cour[z, own, :] * lap + src[t, z, own, :]
                    )
                    done.append(adv)
                for z, adv in zip(range(za, zb), done):
                    nxt[z + HALO, here, :] = adv
                    g = adv * acc[t, z, own, :]
                    grad[xb, z] = g if t == 0 else grad[xb, z] + g
            return 0

        lax.fori_loop(0, rows // TX, block, 0)

    for c in local:
        c.wait()
    mid = [(z, min(z + 8, depth - HALO)) for z in range(HALO, depth - HALO, 8)]
    for t in range(steps):
        for c in per_step[t]:
            c.wait()
        advance(t, mid)
        wait_halos(t)
        advance(t, [(0, HALO), (depth - HALO, depth)])
        if t + 1 < steps:
            start_halos(t + 1)

    out = pltpu.make_async_copy(buf[steps % 2].at[lo:hi, inner, :], last_hbm.at[0], osem)
    out.start()
    places = packed.shape[0]

    def pack(p, _):
        packed[p] = grad[inv_ref[p]]
        pltpu.make_async_copy(packed.at[p], send_hbm.at[p], psem.at[p]).start()
        return 0

    lax.fori_loop(0, places, pack, 0)

    def drain(p, _):
        pltpu.make_async_copy(packed.at[p], send_hbm.at[p], psem.at[p]).wait()
        return 0

    lax.fori_loop(0, places, drain, 0)
    out.wait()


def tile_kernel(
    n_shot, n_sub, send_hbm, ids_hbm, out_hbm,
    recv, rids, tiles, smooth,
    lsem, dsend, drecv, isend, irecv, nsend, nrecv, osem,
):
    shot, sub = lax.axis_index("shot"), lax.axis_index("sub")
    depth, cols = recv.shape[1], recv.shape[3]
    has_up, has_down = sub > 0, sub < n_sub - 1
    barrier = pltpu.get_barrier_semaphore()
    for i in range(1, n_shot):
        pl.semaphore_signal(
            barrier, inc=1, device_id={"shot": lax.rem(shot + i, n_shot)}, device_id_type=MESH
        )

    @pl.when(has_up)
    def _():
        pl.semaphore_signal(barrier, inc=1, device_id={"sub": sub - 1}, device_id_type=MESH)

    @pl.when(has_down)
    def _():
        pl.semaphore_signal(barrier, inc=1, device_id={"sub": sub + 1}, device_id_type=MESH)

    near = jnp.minimum(sub, 1) + jnp.minimum(n_sub - 1 - sub, 1)
    pl.semaphore_wait(barrier, n_shot - 1 + near)

    def part(i):
        return pl.ds(pl.multiple_of(i * CAP, CAP), CAP)

    copies = []
    for i in range(1, n_shot):
        peer = lax.rem(shot + i, n_shot)
        for src, dst, ss, rs in ((ids_hbm, rids, isend, irecv), (send_hbm, recv, dsend, drecv)):
            copies.append(
                pltpu.make_async_remote_copy(
                    src_ref=src.at[part(peer)], dst_ref=dst.at[CAP * i : CAP * (i + 1)],
                    send_sem=ss.at[i], recv_sem=rs.at[i],
                    device_id={"shot": peer}, device_id_type=MESH,
                )
            )
    for c in copies:
        c.start()
    mine = [
        pltpu.make_async_copy(send_hbm.at[part(shot)], recv.at[0:CAP], lsem.at[0]),
        pltpu.make_async_copy(ids_hbm.at[part(shot)], rids.at[0:CAP], lsem.at[1]),
    ]
    for c in mine:
        c.start()

    band_i = lax.broadcasted_iota(jnp.int32, (depth, 3 * depth), 0)
    band_j = lax.broadcasted_iota(jnp.int32, (depth, 3 * depth), 1) - depth
    there = band_j + sub * depth
    gap = band_i - band_j
    ratio = 2.0 * gap.astype(jnp.float32) / depth
    valid = (jnp.abs(gap) <= depth) & (there >= 0) & (there < n_sub * depth)
    band = jnp.where(valid, jnp.exp(-(ratio * ratio)), 0.0)
    band = band / jnp.sum(band, axis=1, keepdims=True)

    @pl.when(jnp.logical_not(has_up))
    def _():
        tiles[:, 0] = jnp.zeros((TILES_OWN, depth * TX, cols), jnp.float32)

    @pl.when(jnp.logical_not(has_down))
    def _():
        tiles[:, 2] = jnp.zeros((TILES_OWN, depth * TX, cols), jnp.float32)

    def gather(blocks, fresh):
        def layer(z, _):
            rows = pl.ds(pl.multiple_of(z * TX, TX), TX)
            data = [recv[p, z] for p in blocks]
            for t in range(TILES_OWN):
                total = None if fresh else tiles[t, 1, rows, :]
                for p, v in zip(blocks, data):
                    term = jnp.where(rids[p] == t, v, 0.0)
                    total = term if total is None else total + term
                tiles[t, 1, rows, :] = total
            return 0

        lax.fori_loop(0, depth, layer, 0)

    for c in mine:
        c.wait()
    gather(range(CAP), True)
    for i in range(1, n_shot):
        copies[2 * i - 2].wait()
        copies[2 * i - 1].wait()
        gather(range(CAP * i, CAP * (i + 1)), False)

    def edge(t):
        up = pltpu.make_async_remote_copy(
            src_ref=tiles.at[t, 1], dst_ref=tiles.at[t, 2],
            send_sem=nsend.at[t, 0], recv_sem=nrecv.at[t, 0],
            device_id={"sub": sub - 1}, device_id_type=MESH,
        )
        down = pltpu.make_async_remote_copy(
            src_ref=tiles.at[t, 1], dst_ref=tiles.at[t, 0],
            send_sem=nsend.at[t, 1], recv_sem=nrecv.at[t, 1],
            device_id={"sub": sub + 1}, device_id_type=MESH,
        )
        return up, down

    def start_edge(t, _):
        up, down = edge(t)

        @pl.when(has_up)
        def _():
            up.start()

        @pl.when(has_down)
        def _():
            down.start()

        return 0

    lax.fori_loop(0, TILES_OWN, start_edge, 0)

    def finish(t, _):
        up, down = edge(t)

        @pl.when(has_up)
        def _():
            up.wait_send()
            down.wait_recv()

        @pl.when(has_down)
        def _():
            down.wait_send()
            up.wait_recv()

        for x in range(TX):
            pencil = jnp.concatenate(
                [tiles[t, s, pl.ds(x, depth, stride=TX), :] for s in range(3)], axis=0
            )
            smooth[t, pl.ds(x, depth, stride=TX), :] = jnp.dot(
                band, pencil, precision=lax.Precision.HIGHEST, preferred_element_type=jnp.float32
            )
        pltpu.make_async_copy(smooth.at[t], out_hbm.at[t], osem.at[t]).start()
        return 0

    lax.fori_loop(0, TILES_OWN, finish, 0)

    def drain(t, _):
        pltpu.make_async_copy(smooth.at[t], out_hbm.at[t], osem.at[t]).wait()
        return 0

    lax.fori_loop(0, TILES_OWN, drain, 0)


def body(courant, adjoint_prev, adjoint_now, forward_accel, traces, receivers, owners, tile_slot):
    n_sub = lax.axis_size("sub")
    n_shot = lax.axis_size("shot")
    _, steps, depth, rows, cols = forward_accel.shape
    places = n_shot * CAP
    f32 = jnp.float32
    smem = pl.BlockSpec(memory_space=pltpu.SMEM)
    vmem = pl.BlockSpec(memory_space=pltpu.VMEM)
    hbm = pl.BlockSpec(memory_space=pl.ANY)

    source, inverse, ids = pl.pallas_call(
        functools.partial(prepare_kernel, depth * rows * cols, cols),
        out_shape=(
            jax.ShapeDtypeStruct((steps, depth * rows, cols), f32),
            jax.ShapeDtypeStruct((places,), jnp.int32),
            jax.ShapeDtypeStruct((places, 8, cols), jnp.int32),
        ),
        in_specs=[smem] * 4,
        out_specs=(vmem, smem, vmem),
        scratch_shapes=[pltpu.SMEM((n_shot,), jnp.int32)],
        compiler_params=pltpu.CompilerParams(vmem_limit_bytes=32 * 2**20),
        name="prepare",
    )(receivers, traces, owners, tile_slot)
    source = source.reshape(steps, depth, rows, cols)

    last, send = pl.pallas_call(
        functools.partial(wave_kernel, n_sub),
        out_shape=(
            jax.ShapeDtypeStruct((1, depth, rows, cols), f32),
            jax.ShapeDtypeStruct((places, depth, TX, cols), f32),
        ),
        in_specs=[smem] + [hbm] * 5,
        out_specs=(hbm, hbm),
        scratch_shapes=[
            pltpu.VMEM((depth + 2 * HALO, rows + 2 * PAD, cols), f32),
            pltpu.VMEM((depth + 2 * HALO, rows + 2 * PAD, cols), f32),
            pltpu.VMEM((depth, rows, cols), f32),
            pltpu.VMEM((steps, depth, rows, cols), f32),
            pltpu.VMEM((steps, depth, rows, cols), f32),
            pltpu.VMEM((rows // TX, depth, TX, cols), f32),
            pltpu.VMEM((places, depth, TX, cols), f32),
            pltpu.SemaphoreType.DMA((3,)),
            pltpu.SemaphoreType.DMA((steps, 2)),
            pltpu.SemaphoreType.DMA((steps, 2)),
            pltpu.SemaphoreType.DMA((steps, 2)),
            pltpu.SemaphoreType.DMA((places,)),
            pltpu.SemaphoreType.DMA,
        ],
        compiler_params=pltpu.CompilerParams(
            collective_id=0, has_side_effects=True, vmem_limit_bytes=48 * 2**20
        ),
        name="wave",
    )(inverse, courant, adjoint_prev, adjoint_now, forward_accel, source)

    smoothed = pl.pallas_call(
        functools.partial(tile_kernel, n_shot, n_sub),
        out_shape=jax.ShapeDtypeStruct((TILES_OWN, depth * TX, cols), f32),
        in_specs=[hbm, hbm],
        out_specs=hbm,
        scratch_shapes=[
            pltpu.VMEM((places, depth, TX, cols), f32),
            pltpu.VMEM((places, 8, cols), jnp.int32),
            pltpu.VMEM((TILES_OWN, 3, depth * TX, cols), f32),
            pltpu.VMEM((TILES_OWN, depth * TX, cols), f32),
            pltpu.SemaphoreType.DMA((2,)),
            pltpu.SemaphoreType.DMA((n_shot,)),
            pltpu.SemaphoreType.DMA((n_shot,)),
            pltpu.SemaphoreType.DMA((n_shot,)),
            pltpu.SemaphoreType.DMA((n_shot,)),
            pltpu.SemaphoreType.DMA((TILES_OWN, 2)),
            pltpu.SemaphoreType.DMA((TILES_OWN, 2)),
            pltpu.SemaphoreType.DMA((TILES_OWN,)),
        ],
        compiler_params=pltpu.CompilerParams(
            collective_id=1, has_side_effects=True, vmem_limit_bytes=32 * 2**20
        ),
        name="tiles",
    )(send, ids)
    return (smoothed.reshape(TILES_OWN, depth, TX, cols), last)


def solution(mesh):
    placed = (
        P("shot", "sub", None, None),
        P("shot", "sub", None, None),
        P("shot", "sub", None, None),
        P("shot", None, "sub", None, None),
        P("shot", None, None),
        P("shot", None),
        P("shot", "sub", None, None),
        P("shot", "sub", None),
    )
    return jax.shard_map(
        body,
        mesh=mesh,
        in_specs=placed,
        out_specs=(P("shot", "sub", None, None), P("shot", "sub", None, None)),
        check_vma=False,
    )
```

profile of v0, /device:TPU:11, one launch (start us, length us, event | category | flops | bytes accessed | tf_op | source)
XLA Modules:
  0.0 123.1 jit_solution(5953758688294729550)
XLA Ops:
  0.6 0.7 copy.10.own_ref
  1.4 0.0 copy-start.1
  1.4 0.7 copy-done.1
  2.1 0.0 copy-start.2
  2.1 0.7 copy-done.2
  2.7 0.0 copy-start.3
  2.7 0.7 copy-done.3
  3.4 9.0 %prepare.1 = (f32[4,4096,128]{2,1,0:T(8,128)S(1)}, s32[16]{0:T(128)S(1)}, s32[16,8,128]{2,1,0:T(8,128)S(1)}) custom-call(s32[1,512]{1,0:T(1,128)S(1)} %copy-done.2, f32[1,4,512]{2,1,0:T(4,128)S(1)} %copy-done.1, s32[1,1,16,1]{3,2,1,0:T(8,128)S(1)} %copy.10.own_ref, s32[1,1,16]{2,1,0:T(1,128)S(1)} %copy-done.3), custom_call_target="tpu_custom_call" | custom-call | tf_op jit(solution)/shard_map/prepare/pallas_call | solution.py:380
  12.4 0.0 copy-start
  12.4 3.2 %copy-done = f32[4,4096,128]{2,1,0:T(8,128)} copy-done((f32[4,4096,128]{2,1,0:T(8,128)}, f32[4,4096,128]{2,1,0:T(8,128)S(1)}, u32[]{:S(2)}) %copy-start) | copy-done | bytes 8388632
  15.7 40.5 %wave.1 = (f32[1,32,128,128]{3,2,1,0:T(8,128)S(1)}, f32[16,32,8,128]{3,2,1,0:T(8,128)S(1)}) custom-call(s32[16]{0:T(128)S(1)} %get-tuple-element.7.inv_ref, f32[1,32,128,128]{3,2,1,0:T(8,128)} %cour_hbm.1, f32[1,32,128,128]{3,2,1,0:T(8,128)} %prev_hbm.1, f32[1,32,128,128]{3,2,1,0:T(8,128)} %now_hbm.1, f32[1,4,32,128,128]{4,3,2,1,0:T(8,128)} %acc_hbm.1, ...), custom_call_target="tpu_custom_call" | custom-call | tf_op jit(solution)/shard_map/wave/pallas_call | solution.py:395
  56.2 64.5 %tiles.1 = f32[8,256,128]{2,1,0:T(8,128)S(1)} custom-call(f32[16,32,8,128]{3,2,1,0:T(8,128)S(1)} %get-tuple-element.9.send_hbm, s32[16,8,128]{2,1,0:T(8,128)S(1)} %get-tuple-element.10.ids_hbm), custom_call_target="tpu_custom_call" | custom-call | tf_op jit(solution)/shard_map/tiles/pallas_call | solution.py:424
  120.8 1.0 copy.13
  121.7 1.3 %copy.14 = f32[1,32,128,128]{3,2,1,0:T(8,128)} copy(f32[1,32,128,128]{3,2,1,0:T(8,128)S(1)} %get-tuple-element.15) | data formatting | bytes 4194304
Async XLA Ops:
  1.4 0.7 copy-start.1
  2.1 0.7 copy-start.2
  2.7 0.7 copy-start.3
  12.4 3.2 %copy-start = (f32[4,4096,128]{2,1,0:T(8,128)}, f32[4,4096,128]{2,1,0:T(8,128)S(1)}, u32[]{:S(2)}) copy-start(f32[4,4096,128]{2,1,0:T(8,128)S(1)} %get-tuple-element.8) | copy-start | bytes 25165828
where the time goes:
time: 124 us; the launch traced here: 123 us
  Pallas kernels  114 us (92%)
  local copies, waits for them, and re-layouts  8.28 us (7%)
    pallas_call x1, Pallas kernels, body(): pl.pallas_call(functools.partial(tile_kernel, n_shot, n_sub), out_shape=j...  64.5 us
    pallas_call x1, Pallas kernels, body(): pl.pallas_call(functools.partial(wave_kernel, n_sub), out_shape=(jax.Shap...  40.5 us
    pallas_call x1, Pallas kernels, body(): pl.pallas_call(functools.partial(prepare_kernel, depth * rows * cols, col...  9.02 us
    unnamed x11, local copies, waits for them, and re-layouts  8.28 us

commit v1 on v0

v1 whole, which is shorter than its diff:
```python
import functools

import jax
import jax.numpy as jnp
from jax import lax
from jax.experimental import pallas as pl
from jax.experimental.pallas import tpu as pltpu
from jax.sharding import PartitionSpec as P

TX = 8
TILES_OWN = 8
CAP = 2
HALO = 4
PAD = 8
UNROLL = 4
MESH = pl.DeviceIdType.MESH

stencil_weights = (-205.0 / 72.0, 8.0 / 5.0, -1.0 / 5.0, 8.0 / 315.0, -1.0 / 560.0)


def prepare_kernel(slab_cells, cols_y, rec_ref, tr_ref, own_ref, slot_ref, src_ref, inv_ref, ids_ref, count_ref):
    steps = tr_ref.shape[1]
    spare = slab_cells // cols_y
    zrows = 256

    def zero(i, _):
        src_ref[pl.ds(pl.multiple_of(i * zrows, zrows), zrows), :] = jnp.zeros((zrows, cols_y), jnp.float32)
        return 0

    lax.fori_loop(0, spare * steps // zrows, zero, 0)
    base = lax.axis_index("sub") * slab_cells
    lane = lax.broadcasted_iota(jnp.int32, (steps, cols_y), 1)
    group = 128

    def add(g, _):
        first = pl.multiple_of(g * group, group)
        values = tr_ref[0, :, pl.ds(first, group)]
        for r in range(group):
            off = rec_ref[0, first + r] - base
            inside = (off >= 0) & (off < slab_cells)
            row = jnp.where(inside, lax.div(off, cols_y), spare)
            at = pl.ds(pl.multiple_of(row * steps, steps), steps)
            value = jnp.broadcast_to(values[:, r : r + 1], (steps, cols_y))
            src_ref[at, :] += jnp.where(lane == lax.rem(off, cols_y), value, 0.0)
        return 0

    lax.fori_loop(0, rec_ref.shape[1] // group, add, 0)

    ids_ref[...] = jnp.full(ids_ref.shape, -1, jnp.int32)
    for i in range(count_ref.shape[0]):
        count_ref[i] = 0
    for i in range(inv_ref.shape[0]):
        inv_ref[i] = 0
    for k in range(slot_ref.shape[0]):
        owner = own_ref[k]
        place = owner * CAP + count_ref[owner]
        count_ref[owner] = count_ref[owner] + 1
        inv_ref[place] = k
        ids_ref[pl.ds(place, 1)] = jnp.full((1,) + ids_ref.shape[1:], slot_ref[k], jnp.int32)


def adjoint_kernel(
    n_shot, n_sub, inv_ref, ids_ref, src_ref, cour_hbm, prev_hbm, now_hbm, acc_hbm,
    last_hbm, out_hbm,
    even, odd, cour, acc, grad, packed, recv, rids, tiles, smooth, taps, scale,
    lsem, asem, hsend, hrecv, isend, irecv, dsend, drecv, nsend, nrecv, fsem, osem,
):
    buf = (even, odd)
    shot, sub = lax.axis_index("shot"), lax.axis_index("sub")
    steps, depth, rows, cols = acc.shape
    places = packed.shape[1]
    chunk = HALO
    chunks = depth // chunk
    inner = pl.ds(PAD, rows)
    rising = lax.rem(sub, 2)
    front, back = sub + 1 - 2 * rising, sub - 1 + 2 * rising
    has_front = (front >= 0) & (front < n_sub)
    has_back = (back >= 0) & (back < n_sub)
    has_low, has_high = sub > 0, sub < n_sub - 1

    def slab(j):
        return chunk * (rising * j + (1 - rising) * (chunks - 1 - j))

    def load(which, j):
        part = pl.ds(slab(j), chunk)
        inside = pl.ds(slab(j) + HALO, chunk)
        if which == 0:
            return pltpu.make_async_copy(now_hbm.at[0, part], even.at[inside, inner, :], lsem.at[0, j])
        if which == 1:
            return pltpu.make_async_copy(prev_hbm.at[0, part], odd.at[inside, inner, :], lsem.at[1, j])
        return pltpu.make_async_copy(cour_hbm.at[0, part], cour.at[part], lsem.at[2, j])

    def load_acc(t, j):
        part = pl.ds(slab(j), chunk)
        return pltpu.make_async_copy(acc_hbm.at[0, t, part], acc.at[t, part], asem.at[t, j])

    load(0, 0).start()
    for i in range(chunks + steps - 1):
        for t in range(steps):
            j = i - t
            if 0 <= j < chunks:
                if t == 0:
                    if j + 1 < chunks:
                        load(0, j + 1).start()
                    load(1, j).start()
                    load(2, j).start()
                load_acc(t, j).start()

    barrier = pltpu.get_barrier_semaphore()

    def peer_of(m):
        return lax.rem(shot + m, n_shot)

    for m in range(1, n_shot):
        pl.semaphore_signal(barrier, inc=1, device_id={"shot": peer_of(m)}, device_id_type=MESH)

    @pl.when(has_front)
    def _():
        pl.semaphore_signal(barrier, inc=1, device_id={"sub": front}, device_id_type=MESH)

    @pl.when(has_back)
    def _():
        pl.semaphore_signal(barrier, inc=1, device_id={"sub": back}, device_id_type=MESH)

    for ref in buf:
        for rim in (0, PAD + rows):
            ref[HALO : HALO + depth, rim : rim + PAD, :] = jnp.zeros((depth, PAD, cols), jnp.float32)

    def clear(first):
        for ref in buf:
            ref[first : first + HALO, inner, :] = jnp.zeros((HALO, rows, cols), jnp.float32)

    @pl.when(jnp.logical_not(has_low))
    def _():
        clear(0)

    @pl.when(jnp.logical_not(has_high))
    def _():
        clear(HALO + depth)

    near = jnp.minimum(sub, 1) + jnp.minimum(n_sub - 1 - sub, 1)
    pl.semaphore_wait(barrier, n_shot - 1 + near)

    def halo(t, side):
        b = buf[t % 2]
        if side == 0:
            first, land, device = (1 - rising) * (depth - HALO), rising * (depth + HALO), front
        else:
            first, land, device = rising * (depth - HALO), (1 - rising) * (depth + HALO), back
        source = now_hbm.at[0, pl.ds(first, HALO)] if t == 0 else b.at[pl.ds(first + HALO, HALO), inner, :]
        return pltpu.make_async_remote_copy(
            src_ref=source, dst_ref=b.at[pl.ds(land, HALO), inner, :],
            send_sem=hsend.at[t, side], recv_sem=hrecv.at[t, side],
            device_id={"sub": device}, device_id_type=MESH,
        )

    there = (has_front, has_back)

    def start_halo(t, side):
        @pl.when(there[side])
        def _():
            halo(t, side).start()

    def wait_halo(t, side):
        @pl.when(there[side])
        def _():
            halo(t, side).wait()

    start_halo(0, 0)
    start_halo(0, 1)

    def ids_copy(m):
        peer = peer_of(m)
        return pltpu.make_async_remote_copy(
            src_ref=ids_ref.at[pl.ds(CAP * peer, CAP)], dst_ref=rids.at[pl.ds(CAP * m, CAP)],
            send_sem=isend.at[m], recv_sem=irecv.at[m],
            device_id={"shot": peer}, device_id_type=MESH,
        )

    def data_copy(j, m):
        peer = peer_of(m)
        return pltpu.make_async_remote_copy(
            src_ref=packed.at[j, pl.ds(CAP * peer, CAP)], dst_ref=recv.at[j, pl.ds(CAP * m, CAP)],
            send_sem=dsend.at[j, m], recv_sem=drecv.at[j, m],
            device_id={"shot": peer}, device_id_type=MESH,
        )

    for m in range(1, n_shot):
        ids_copy(m).start()

    lane = lax.broadcasted_iota(jnp.int32, (TX, cols), 1)
    from_left = [None] + [jnp.where(lane >= d, stencil_weights[d], 0.0) for d in range(1, 5)]
    from_right = [None] + [jnp.where(lane < cols - d, stencil_weights[d], 0.0) for d in range(1, 5)]

    def advance(t, j):
        cur, nxt = buf[t % 2], buf[(t + 1) % 2]
        z0 = slab(j)

        def block(i, _):
            for u in range(UNROLL):
                xb = i * UNROLL + u
                x0 = pl.multiple_of(xb * TX, TX)
                own = pl.ds(x0, TX)
                here = pl.ds(pl.multiple_of(x0 + PAD, TX), TX)
                col = {k: cur[z0 + (k + HALO), here, :] for k in range(-HALO, chunk + HALO)}
                for k in range(chunk):
                    z = z0 + k
                    c = col[k]
                    lap = (3.0 * stencil_weights[0]) * c
                    for d in range(1, 5):
                        pair = (col[k + d] + col[k - d]) + (
                            cur[z + HALO, pl.ds(x0 + (PAD + d), TX), :]
                            + cur[z + HALO, pl.ds(x0 + (PAD - d), TX), :]
                        )
                        lap = lap + stencil_weights[d] * pair
                        lap = lap + from_left[d] * pltpu.roll(c, d, 1)
                        lap = lap + from_right[d] * pltpu.roll(c, cols - d, 1)
                    source = src_ref[pl.ds((z * rows + x0) * steps + t, TX, stride=steps), :]
                    adv = (2.0 * c - nxt[z + HALO, here, :]) + (cour[z, own, :] * lap + source)
                    nxt[z + HALO, here, :] = adv
                    g = adv * acc[t, z, own, :]
                    grad[xb, z] = g if t == 0 else grad[xb, z] + g
            return 0

        lax.fori_loop(0, rows // (TX * UNROLL), block, 0)

    def last_copy(j):
        part = pl.ds(slab(j), chunk)
        return pltpu.make_async_copy(
            buf[steps % 2].at[pl.ds(slab(j) + HALO, chunk), inner, :], last_hbm.at[0, part], fsem.at[j]
        )

    def send(j):
        part = pl.ds(slab(j), chunk)

        def pack(p, _):
            packed[j, p] = grad[inv_ref[p], part]
            return 0

        lax.fori_loop(0, places, pack, 0, unroll=4)
        for m in range(1, n_shot):
            data_copy(j, m).start()

    load(0, 0).wait()

    def sweep(i, _):
        for t in range(steps):
            j = i - t

            @pl.when((j >= 0) & (j < chunks))
            def _():
                if t == 0:
                    @pl.when(j + 1 < chunks)
                    def _():
                        load(0, j + 1).wait()

                    load(1, j).wait()
                    load(2, j).wait()
                load_acc(t, j).wait()

                @pl.when(j == 0)
                def _():
                    wait_halo(t, 0)

                @pl.when(j == chunks - 1)
                def _():
                    wait_halo(t, 1)

                advance(t, j)
                if t + 1 < steps:
                    @pl.when(j == 0)
                    def _():
                        start_halo(t + 1, 0)

                    @pl.when(j == chunks - 1)
                    def _():
                        start_halo(t + 1, 1)
                else:
                    send(j)
                    last_copy(j).start()

        return 0

    lax.fori_loop(0, chunks + steps - 1, sweep, 0)

    far = lax.broadcasted_iota(jnp.int32, taps.shape, 0).astype(jnp.float32)
    ratio = 2.0 * far / depth
    taps[...] = jnp.exp(-(ratio * ratio))
    row_i = lax.broadcasted_iota(jnp.int32, (depth, 3 * depth), 0)
    row_j = lax.broadcasted_iota(jnp.int32, (depth, 3 * depth), 1) - depth
    gap = row_i - row_j
    whole = row_j + sub * depth
    ratio = 2.0 * gap.astype(jnp.float32) / depth
    valid = (jnp.abs(gap) <= depth) & (whole >= 0) & (whole < n_sub * depth)
    total = jnp.sum(jnp.where(valid, jnp.exp(-(ratio * ratio)), 0.0), axis=1, keepdims=True)
    scale[...] = jnp.broadcast_to(1.0 / total, scale.shape)
    smooth[...] = jnp.zeros(smooth.shape, jnp.float32)

    def spread(first, low, high):
        def row(i, _):
            w = []
            for k in range(chunk):
                gap = i - (first + k - depth)
                away = jnp.maximum(gap, -gap)
                w.append(jnp.where(away <= depth, taps[jnp.minimum(away, depth)], 0.0))
            for g in range(TILES_OWN):
                s = smooth[g, i]
                for k in range(chunk):
                    s = s + w[k] * tiles[first + k, g]
                smooth[g, i] = s
            return 0

        lax.fori_loop(low, high, row, 0)

    def collect(j):
        z0 = slab(j)

        def tile(g, _):
            sums = [None] * chunk
            for p in range(places):
                if p < CAP:
                    hit = ids_ref[CAP * shot + p] == g
                    block = [packed[j, CAP * shot + p, k] for k in range(chunk)]
                else:
                    hit = rids[p] == g
                    block = [recv[j, p, k] for k in range(chunk)]
                for k in range(chunk):
                    term = jnp.where(hit, block[k], 0.0)
                    sums[k] = term if sums[k] is None else sums[k] + term
            for k in range(chunk):
                tiles[depth + z0 + k, g] = sums[k]
            return 0

        lax.fori_loop(0, TILES_OWN, tile, 0)

    def pass_on(j, side):
        z0 = slab(j)
        land, device = (2 * depth + z0, sub - 1) if side == 0 else (z0, sub + 1)
        return pltpu.make_async_remote_copy(
            src_ref=tiles.at[pl.ds(depth + z0, chunk)], dst_ref=tiles.at[pl.ds(land, chunk)],
            send_sem=nsend.at[j, side], recv_sem=nrecv.at[j, side],
            device_id={"sub": device}, device_id_type=MESH,
        )

    def finish(j):
        z0 = chunk * (chunks - 1) - slab(j)

        @pl.when(has_low)
        def _():
            pass_on(j, 0).wait_send()
            pass_on(j, 1).wait_recv()
            spread(z0, 0, z0 + chunk)

        @pl.when(has_high)
        def _():
            pass_on(j, 1).wait_send()
            pass_on(j, 0).wait_recv()
            spread(2 * depth + z0, z0, depth)

    for m in range(1, n_shot):
        ids_copy(m).wait()

    def gather(j, _):
        for m in range(1, n_shot):
            data_copy(j, m).wait()
        collect(j)

        @pl.when(has_low)
        def _():
            pass_on(j, 0).start()

        @pl.when(has_high)
        def _():
            pass_on(j, 1).start()

        spread(depth + slab(j), 0, depth)

        @pl.when(j > 0)
        def _():
            finish(j - 1)

        return 0

    lax.fori_loop(0, chunks, gather, 0)
    finish(chunks - 1)

    def normal(i, _):
        s = scale[pl.ds(i, TX, stride=0), :]
        for g in range(TILES_OWN):
            smooth[g, i] = smooth[g, i] * s
        return 0

    lax.fori_loop(0, depth, normal, 0)
    done = pltpu.make_async_copy(smooth, out_hbm, osem)
    done.start()
    for j in range(chunks):
        last_copy(j).wait()
    done.wait()


def body(courant, adjoint_prev, adjoint_now, forward_accel, traces, receivers, owners, tile_slot):
    n_sub = lax.axis_size("sub")
    n_shot = lax.axis_size("shot")
    _, steps, depth, rows, cols = forward_accel.shape
    places = n_shot * CAP
    chunks = depth // HALO
    f32 = jnp.float32
    smem = pl.BlockSpec(memory_space=pltpu.SMEM)
    vmem = pl.BlockSpec(memory_space=pltpu.VMEM)
    hbm = pl.BlockSpec(memory_space=pl.ANY)

    source, inverse, ids = pl.pallas_call(
        functools.partial(prepare_kernel, depth * rows * cols, cols),
        out_shape=(
            jax.ShapeDtypeStruct(((depth * rows + 2) * steps, cols), f32),
            jax.ShapeDtypeStruct((places,), jnp.int32),
            jax.ShapeDtypeStruct((places, TX, cols), jnp.int32),
        ),
        in_specs=[smem, vmem, smem, smem],
        out_specs=(vmem, smem, vmem),
        scratch_shapes=[pltpu.SMEM((n_shot,), jnp.int32)],
        compiler_params=pltpu.CompilerParams(vmem_limit_bytes=32 * 2**20),
        name="prepare",
    )(receivers, traces, owners.reshape(-1), tile_slot.reshape(-1))

    last, smoothed = pl.pallas_call(
        functools.partial(adjoint_kernel, n_shot, n_sub),
        out_shape=(
            jax.ShapeDtypeStruct((1, depth, rows, cols), f32),
            jax.ShapeDtypeStruct((TILES_OWN, depth, TX, cols), f32),
        ),
        in_specs=[smem, vmem, vmem] + [hbm] * 4,
        out_specs=(hbm, hbm),
        scratch_shapes=[
            pltpu.VMEM((depth + 2 * HALO, rows + 2 * PAD, cols), f32),
            pltpu.VMEM((depth + 2 * HALO, rows + 2 * PAD, cols), f32),
            pltpu.VMEM((depth, rows, cols), f32),
            pltpu.VMEM((steps, depth, rows, cols), f32),
            pltpu.VMEM((rows // TX, depth, TX, cols), f32),
            pltpu.VMEM((chunks, places, HALO, TX, cols), f32),
            pltpu.VMEM((chunks, places, HALO, TX, cols), f32),
            pltpu.VMEM((places, TX, cols), jnp.int32),
            pltpu.VMEM((3 * depth, TILES_OWN, TX, cols), f32),
            pltpu.VMEM((TILES_OWN, depth, TX, cols), f32),
            pltpu.VMEM((depth + 1, TX, cols), f32),
            pltpu.VMEM((depth, cols), f32),
            pltpu.SemaphoreType.DMA((3, chunks)),
            pltpu.SemaphoreType.DMA((steps, chunks)),
            pltpu.SemaphoreType.DMA((steps, 2)),
            pltpu.SemaphoreType.DMA((steps, 2)),
            pltpu.SemaphoreType.DMA((n_shot,)),
            pltpu.SemaphoreType.DMA((n_shot,)),
            pltpu.SemaphoreType.DMA((chunks, n_shot)),
            pltpu.SemaphoreType.DMA((chunks, n_shot)),
            pltpu.SemaphoreType.DMA((chunks, 2)),
            pltpu.SemaphoreType.DMA((chunks, 2)),
            pltpu.SemaphoreType.DMA((chunks,)),
            pltpu.SemaphoreType.DMA,
        ],
        compiler_params=pltpu.CompilerParams(
            collective_id=0, has_side_effects=True, vmem_limit_bytes=40 * 2**20
        ),
        name="adjoint",
    )(inverse, ids, source, courant, adjoint_prev, adjoint_now, forward_accel)
    return (smoothed, last)


def solution(mesh):
    placed = (
        P("shot", "sub", None, None),
        P("shot", "sub", None, None),
        P("shot", "sub", None, None),
        P("shot", None, "sub", None, None),
        P("shot", None, None),
        P("shot", None),
        P("shot", "sub", None, None),
        P("shot", "sub", None),
    )
    return jax.shard_map(
        body,
        mesh=mesh,
        in_specs=placed,
        out_specs=(P("shot", "sub", None, None), P("shot", "sub", None, None)),
        check_vma=False,
    )
```

time: 124 us -> 92.5 us (0.75)
  Pallas kernels: 114 us -> 77.6 us
  local copies, waits for them, and re-layouts: 8.28 us -> 13 us
    pallas_call x2 -> x1, Pallas kernels: 105 us -> 72.6 us  [body(): pl.pallas_call(functools.partial(adjoint_kernel, n_shot, n_sub), out_shap...]
    unnamed x11 -> x18, local copies, waits for them, and re-layouts: 8.28 us -> 13 us
    pallas_call x1, Pallas kernels: 9.02 us -> 4.96 us  [body(): pl.pallas_call(functools.partial(prepare_kernel, depth * rows * cols, col...]
where the time goes in v1:
time: 92.5 us; the launch traced here: 91.2 us
  Pallas kernels  77.6 us (84%)
  local copies, waits for them, and re-layouts  13 us (14%)
    pallas_call x1, Pallas kernels, body(): pl.pallas_call(functools.partial(adjoint_kernel, n_shot, n_sub), out_shap...  72.6 us
    unnamed x18, local copies, waits for them, and re-layouts  13 us
    pallas_call x1, Pallas kernels, body(): pl.pallas_call(functools.partial(prepare_kernel, depth * rows * cols, col...  4.96 us

profile of v1, /device:TPU:11, one launch (start us, length us, event | category | flops | bytes accessed | tf_op | source)
XLA Modules:
  0.0 91.2 jit_solution(4667227329036184125)
XLA Ops:
  0.6 0.0 copy-start.4
  0.6 0.7 copy-done.4
  1.3 0.0 copy-start.5
  1.3 0.7 copy-done.5
  2.0 0.0 copy-start.6
  2.0 0.7 copy-done.6
  2.7 0.0 copy-start.7
  2.7 0.7 copy-done.7
  3.3 5.0 %prepare.1 = (f32[16392,128]{1,0:T(8,128)S(1)}, s32[16]{0:T(128)S(1)}, s32[16,8,128]{2,1,0:T(8,128)S(1)}) custom-call(s32[1,512]{1,0:T(1,128)S(1)} %copy-done.5, f32[1,4,512]{2,1,0:T(4,128)S(1)} %copy-done.4, s32[16]{0:T(128)S(1)} %bitcast.2, s32[16]{0:T(128)S(1)} %bitcast.3), custom_call_target="tpu_custom_call" | custom-call | tf_op jit(solution)/shard_map/prepare/pallas_call | solution.py:412
  8.3 0.0 copy-start
  8.3 3.2 %copy-done = f32[16392,128]{1,0:T(8,128)} copy-done((f32[16392,128]{1,0:T(8,128)}, f32[16392,128]{1,0:T(8,128)S(1)}, u32[]{:S(2)}) %copy-start) | copy-done | bytes 8392728
  11.5 0.0 copy-start.1
  11.5 1.6 %copy-done.1 = f32[1,32,128,128]{3,2,1,0:T(8,128)S(1)} copy-done((f32[1,32,128,128]{3,2,1,0:T(8,128)S(1)}, f32[1,32,128,128]{3,2,1,0:T(8,128)}, u32[]{:S(2)}) %copy-start.1) | copy-done | bytes 2097176
  13.1 0.0 copy-start.2
  13.1 1.6 %copy-done.2 = f32[1,32,128,128]{3,2,1,0:T(8,128)S(1)} copy-done((f32[1,32,128,128]{3,2,1,0:T(8,128)S(1)}, f32[1,32,128,128]{3,2,1,0:T(8,128)}, u32[]{:S(2)}) %copy-start.2) | copy-done | bytes 2097176
  14.7 0.0 copy-start.3
  14.7 1.6 %copy-done.3 = f32[1,32,128,128]{3,2,1,0:T(8,128)S(1)} copy-done((f32[1,32,128,128]{3,2,1,0:T(8,128)S(1)}, f32[1,32,128,128]{3,2,1,0:T(8,128)}, u32[]{:S(2)}) %copy-start.3) | copy-done | bytes 2097176
  16.3 72.6 %adjoint.1 = (f32[1,32,128,128]{3,2,1,0:T(8,128)S(1)}, f32[8,32,8,128]{3,2,1,0:T(8,128)S(1)}) custom-call(s32[16]{0:T(128)S(1)} %get-tuple-element.7.inv_ref, s32[16,8,128]{2,1,0:T(8,128)S(1)} %get-tuple-element.8.ids_ref, f32[16392,128]{1,0:T(8,128)} %copy-done, f32[1,32,128,128]{3,2,1,0:T(8,128)S(1)} %copy-done.1, f32[1,32,128,128]{3,2,1,0:T(8,128)S(1)} %copy-done.2, ...), custom_call_target="tpu_custom_call" | custom-call | tf_op jit(solution)/shard_map/adjoint/pallas_call | solution.py:426
  88.9 1.0 %copy.12 = f32[8,32,8,128]{3,2,1,0:T(8,128)} copy(f32[8,32,8,128]{3,2,1,0:T(8,128)S(1)} %get-tuple-element.14) | data formatting | bytes 2097152
  89.9 1.3 %copy.13 = f32[1,32,128,128]{3,2,1,0:T(8,128)} copy(f32[1,32,128,128]{3,2,1,0:T(8,128)S(1)} %get-tuple-element.15) | data formatting | bytes 4194304
Async XLA Ops:
  0.6 0.7 copy-start.4
  1.3 0.7 copy-start.5
  2.0 0.7 copy-start.6
  2.7 0.7 copy-start.7
  8.3 3.2 %copy-start = (f32[16392,128]{1,0:T(8,128)}, f32[16392,128]{1,0:T(8,128)S(1)}, u32[]{:S(2)}) copy-start(f32[16392,128]{1,0:T(8,128)S(1)} %get-tuple-element.9.src_ref) | copy-start | bytes 25178116
  11.5 1.6 %copy-start.1 = (f32[1,32,128,128]{3,2,1,0:T(8,128)S(1)}, f32[1,32,128,128]{3,2,1,0:T(8,128)}, u32[]{:S(2)}) copy-start(f32[1,32,128,128]{3,2,1,0:T(8,128)} %cour_hbm.1) | copy-start | bytes 6291460
  13.1 1.6 %copy-start.2 = (f32[1,32,128,128]{3,2,1,0:T(8,128)S(1)}, f32[1,32,128,128]{3,2,1,0:T(8,128)}, u32[]{:S(2)}) copy-start(f32[1,32,128,128]{3,2,1,0:T(8,128)} %prev_hbm.1) | copy-start | bytes 6291460
  14.7 1.6 %copy-start.3 = (f32[1,32,128,128]{3,2,1,0:T(8,128)S(1)}, f32[1,32,128,128]{3,2,1,0:T(8,128)}, u32[]{:S(2)}) copy-start(f32[1,32,128,128]{3,2,1,0:T(8,128)} %now_hbm.1) | copy-start | bytes 6291460

commit v2 on v1

--- a/solution.py
+++ b/solution.py
@@ -18,7 +18,18 @@
 stencil_weights = (-205.0 / 72.0, 8.0 / 5.0, -1.0 / 5.0, 8.0 / 315.0, -1.0 / 560.0)
 
 
-def prepare_kernel(slab_cells, cols_y, rec_ref, tr_ref, own_ref, slot_ref, src_ref, inv_ref, ids_ref, count_ref):
+def prepare_kernel(
+    slab_cells, cols_y, rec_hbm, tr_hbm, own_hbm, slot_hbm, src_ref, inv_ref, ids_ref,
+    count_ref, rec_ref, tr_ref, own_ref, slot_ref, sems,
+):
+    arrivals = [
+        pltpu.make_async_copy(a, b, sems.at[i])
+        for i, (a, b) in enumerate(
+            ((rec_hbm, rec_ref), (tr_hbm, tr_ref), (own_hbm, own_ref), (slot_hbm, slot_ref))
+        )
+    ]
+    for c in arrivals:
+        c.start()
     steps = tr_ref.shape[1]
     spare = slab_cells // cols_y
     zrows = 256
@@ -28,6 +39,9 @@
         return 0
 
     lax.fori_loop(0, spare * steps // zrows, zero, 0)
+    ids_ref[...] = jnp.full(ids_ref.shape, -1, jnp.int32)
+    for c in arrivals:
+        c.wait()
     base = lax.axis_index("sub") * slab_cells
     lane = lax.broadcasted_iota(jnp.int32, (steps, cols_y), 1)
     group = 128
@@ -46,7 +60,6 @@
 
     lax.fori_loop(0, rec_ref.shape[1] // group, add, 0)
 
-    ids_ref[...] = jnp.full(ids_ref.shape, -1, jnp.int32)
     for i in range(count_ref.shape[0]):
         count_ref[i] = 0
     for i in range(inv_ref.shape[0]):
@@ -61,9 +74,9 @@
 
 def adjoint_kernel(
     n_shot, n_sub, inv_ref, ids_ref, src_ref, cour_hbm, prev_hbm, now_hbm, acc_hbm,
-    last_hbm, out_hbm,
-    even, odd, cour, acc, grad, packed, recv, rids, tiles, smooth, taps, scale,
-    lsem, asem, hsend, hrecv, isend, irecv, dsend, drecv, nsend, nrecv, fsem, osem,
+    last, smooth,
+    even, odd, cour, acc, grad, packed, recv, rids, tiles, taps, scale,
+    lsem, asem, hsend, hrecv, isend, irecv, dsend, drecv, nsend, nrecv,
 ):
     buf = (even, odd)
     shot, sub = lax.axis_index("shot"), lax.axis_index("sub")
@@ -217,18 +230,15 @@
                         lap = lap + from_right[d] * pltpu.roll(c, cols - d, 1)
                     source = src_ref[pl.ds((z * rows + x0) * steps + t, TX, stride=steps), :]
                     adv = (2.0 * c - nxt[z + HALO, here, :]) + (cour[z, own, :] * lap + source)
-                    nxt[z + HALO, here, :] = adv
+                    if t + 1 < steps:
+                        nxt[z + HALO, here, :] = adv
+                    else:
+                        last[0, z, own, :] = adv
                     g = adv * acc[t, z, own, :]
                     grad[xb, z] = g if t == 0 else grad[xb, z] + g
             return 0
 
         lax.fori_loop(0, rows // (TX * UNROLL), block, 0)
-
-    def last_copy(j):
-        part = pl.ds(slab(j), chunk)
-        return pltpu.make_async_copy(
-            buf[steps % 2].at[pl.ds(slab(j) + HALO, chunk), inner, :], last_hbm.at[0, part], fsem.at[j]
-        )
 
     def send(j):
         part = pl.ds(slab(j), chunk)
@@ -277,7 +287,6 @@
                         start_halo(t + 1, 1)
                 else:
                     send(j)
-                    last_copy(j).start()
 
         return 0
 
@@ -391,11 +400,17 @@
         return 0
 
     lax.fori_loop(0, depth, normal, 0)
-    done = pltpu.make_async_copy(smooth, out_hbm, osem)
-    done.start()
-    for j in range(chunks):
-        last_copy(j).wait()
-    done.wait()
+
+
+def store_kernel(smooth_ref, last_ref, smooth_hbm, last_hbm, sems):
+    copies = [
+        pltpu.make_async_copy(last_ref, last_hbm, sems.at[0]),
+        pltpu.make_async_copy(smooth_ref, smooth_hbm, sems.at[1]),
+    ]
+    for c in copies:
+        c.start()
+    for c in copies:
+        c.wait()
 
 
 def body(courant, adjoint_prev, adjoint_now, forward_accel, traces, receivers, owners, tile_slot):
@@ -409,28 +424,41 @@
     vmem = pl.BlockSpec(memory_space=pltpu.VMEM)
     hbm = pl.BlockSpec(memory_space=pl.ANY)
 
+    def in_hbm(x):
+        return pltpu.with_memory_space_constraint(x, pltpu.HBM)
+
+    def in_vmem(x):
+        return pltpu.with_memory_space_constraint(x, pltpu.VMEM)
+
     source, inverse, ids = pl.pallas_call(
         functools.partial(prepare_kernel, depth * rows * cols, cols),
         out_shape=(
-            jax.ShapeDtypeStruct(((depth * rows + 2) * steps, cols), f32),
+            pltpu.VMEM(((depth * rows + 2) * steps, cols), f32),
             jax.ShapeDtypeStruct((places,), jnp.int32),
-            jax.ShapeDtypeStruct((places, TX, cols), jnp.int32),
+            pltpu.VMEM((places, TX, cols), jnp.int32),
         ),
-        in_specs=[smem, vmem, smem, smem],
+        in_specs=[hbm] * 4,
         out_specs=(vmem, smem, vmem),
-        scratch_shapes=[pltpu.SMEM((n_shot,), jnp.int32)],
+        scratch_shapes=[
+            pltpu.SMEM((n_shot,), jnp.int32),
+            pltpu.SMEM(receivers.shape, jnp.int32),
+            pltpu.VMEM(traces.shape, f32),
+            pltpu.SMEM((owners.size,), jnp.int32),
+            pltpu.SMEM((tile_slot.size,), jnp.int32),
+            pltpu.SemaphoreType.DMA((4,)),
+        ],
         compiler_params=pltpu.CompilerParams(vmem_limit_bytes=32 * 2**20),
         name="prepare",
-    )(receivers, traces, owners.reshape(-1), tile_slot.reshape(-1))
+    )(*(in_hbm(x) for x in (receivers, traces, owners.reshape(-1), tile_slot.reshape(-1))))
 
     last, smoothed = pl.pallas_call(
         functools.partial(adjoint_kernel, n_shot, n_sub),
         out_shape=(
-            jax.ShapeDtypeStruct((1, depth, rows, cols), f32),
-            jax.ShapeDtypeStruct((TILES_OWN, depth, TX, cols), f32),
+            pltpu.VMEM((1, depth, rows, cols), f32),
+            pltpu.VMEM((TILES_OWN, depth, TX, cols), f32),
         ),
         in_specs=[smem, vmem, vmem] + [hbm] * 4,
-        out_specs=(hbm, hbm),
+        out_specs=(vmem, vmem),
         scratch_shapes=[
             pltpu.VMEM((depth + 2 * HALO, rows + 2 * PAD, cols), f32),
             pltpu.VMEM((depth + 2 * HALO, rows + 2 * PAD, cols), f32),
@@ -441,7 +469,6 @@
             pltpu.VMEM((chunks, places, HALO, TX, cols), f32),
             pltpu.VMEM((places, TX, cols), jnp.int32),
             pltpu.VMEM((3 * depth, TILES_OWN, TX, cols), f32),
-            pltpu.VMEM((TILES_OWN, depth, TX, cols), f32),
             pltpu.VMEM((depth + 1, TX, cols), f32),
             pltpu.VMEM((depth, cols), f32),
             pltpu.SemaphoreType.DMA((3, chunks)),
@@ -454,14 +481,24 @@
             pltpu.SemaphoreType.DMA((chunks, n_shot)),
             pltpu.SemaphoreType.DMA((chunks, 2)),
             pltpu.SemaphoreType.DMA((chunks, 2)),
-            pltpu.SemaphoreType.DMA((chunks,)),
-            pltpu.SemaphoreType.DMA,
         ],
         compiler_params=pltpu.CompilerParams(
             collective_id=0, has_side_effects=True, vmem_limit_bytes=40 * 2**20
         ),
         name="adjoint",
-    )(inverse, ids, source, courant, adjoint_prev, adjoint_now, forward_accel)
+    )(
+        inverse, in_vmem(ids), in_vmem(source),
+        *(in_hbm(x) for x in (courant, adjoint_prev, adjoint_now, forward_accel)),
+    )
+
+    smoothed, last = pl.pallas_call(
+        store_kernel,
+        out_shape=tuple(pltpu.HBM(x.shape, f32) for x in (smoothed, last)),
+        in_specs=[hbm, hbm],
+        out_specs=(hbm, hbm),
+        scratch_shapes=[pltpu.SemaphoreType.DMA((2,))],
+        name="store",
+    )(in_vmem(smoothed), in_vmem(last))
     return (smoothed, last)
 
 

time: 92.5 us -> 77.7 us (0.84)
  local copies, waits for them, and re-layouts: 13 us -> 0 us
  Pallas kernels: 77.6 us -> 75.8 us
    unnamed x18 -> x0, local copies, waits for them, and re-layouts: 13 us -> none
    pallas_call x1, Pallas kernels: 72.6 us -> 69.5 us  [body(): pl.pallas_call(functools.partial(adjoint_kernel, n_shot, n_sub), out_shap...]
    pallas_call x0 -> x1, Pallas kernels: none -> 1.68 us  [body(): pl.pallas_call(store_kernel, out_shape=tuple((pltpu.HBM(x.shape, f32) for...]
where the time goes in v2:
time: 77.7 us; the launch traced here: 76.5 us
  Pallas kernels  75.8 us (98%)
    pallas_call x1, Pallas kernels, body(): pl.pallas_call(functools.partial(adjoint_kernel, n_shot, n_sub), out_shap...  69.5 us
    pallas_call x1, Pallas kernels, body(): pl.pallas_call(functools.partial(prepare_kernel, depth * rows * cols, col...  4.66 us
    pallas_call x1, Pallas kernels, body(): pl.pallas_call(store_kernel, out_shape=tuple((pltpu.HBM(x.shape, f32) for...  1.68 us

profile of v2, /device:TPU:11, one launch (start us, length us, event | category | flops | bytes accessed | tf_op | source)
XLA Modules:
  0.0 76.5 jit_solution(7094564761334894818)
XLA Ops:
  0.6 4.7 %prepare.1 = (f32[16392,128]{1,0:T(8,128)S(1)}, s32[16]{0:T(128)S(1)}, s32[16,8,128]{2,1,0:T(8,128)S(1)}) custom-call(s32[1,512]{1,0:T(1,128)} %rec_hbm.1, f32[1,4,512]{2,1,0:T(4,128)} %tr_hbm.1, s32[16]{0:T(128)} %bitcast.2, s32[16]{0:T(128)} %bitcast.3), custom_call_target="tpu_custom_call" | custom-call | tf_op jit(solution)/shard_map/prepare/pallas_call | solution.py:433
  5.3 69.5 %adjoint.1 = (f32[1,32,128,128]{3,2,1,0:T(8,128)S(1)}, f32[8,32,8,128]{3,2,1,0:T(8,128)S(1)}) custom-call(s32[16]{0:T(128)S(1)} %get-tuple-element.7.inv_ref, s32[16,8,128]{2,1,0:T(8,128)S(1)} %get-tuple-element.8.ids_ref, f32[16392,128]{1,0:T(8,128)S(1)} %get-tuple-element.9.src_ref, f32[1,32,128,128]{3,2,1,0:T(8,128)} %cour_hbm.1, ...), custom_call_target="tpu_custom_call" | custom-call | tf_op jit(solution)/shard_map/adjoint/pallas_call | solution.py:454
  74.8 1.7 %store.1 = (f32[8,32,8,128]{3,2,1,0:T(8,128)}, f32[1,32,128,128]{3,2,1,0:T(8,128)}) custom-call(f32[8,32,8,128]{3,2,1,0:T(8,128)S(1)} %get-tuple-element.10.smooth_ref, f32[1,32,128,128]{3,2,1,0:T(8,128)S(1)} %get-tuple-element.11.last_ref), custom_call_target="tpu_custom_call" | custom-call | tf_op jit(solution)/shard_map/store/pallas_call | solution.py:494

commit v3 on v2

--- a/solution.py
+++ b/solution.py
@@ -12,7 +12,7 @@
 CAP = 2
 HALO = 4
 PAD = 8
-UNROLL = 4
+UNROLL = 8
 MESH = pl.DeviceIdType.MESH
 
 stencil_weights = (-205.0 / 72.0, 8.0 / 5.0, -1.0 / 5.0, 8.0 / 315.0, -1.0 / 560.0)
@@ -32,6 +32,8 @@
         c.start()
     steps = tr_ref.shape[1]
     spare = slab_cells // cols_y
+    shift = cols_y.bit_length() - 1
+    assert cols_y == 1 << shift
     zrows = 256
 
     def zero(i, _):
@@ -51,11 +53,11 @@
         values = tr_ref[0, :, pl.ds(first, group)]
         for r in range(group):
             off = rec_ref[0, first + r] - base
-            inside = (off >= 0) & (off < slab_cells)
-            row = jnp.where(inside, lax.div(off, cols_y), spare)
+            row = jnp.right_shift(off, shift)
+            row = jnp.minimum(row.astype(jnp.uint32), jnp.uint32(spare)).astype(jnp.int32)
             at = pl.ds(pl.multiple_of(row * steps, steps), steps)
             value = jnp.broadcast_to(values[:, r : r + 1], (steps, cols_y))
-            src_ref[at, :] += jnp.where(lane == lax.rem(off, cols_y), value, 0.0)
+            src_ref[at, :] += jnp.where(lane == jnp.bitwise_and(off, cols_y - 1), value, 0.0)
         return 0
 
     lax.fori_loop(0, rec_ref.shape[1] // group, add, 0)
@@ -75,8 +77,8 @@
 def adjoint_kernel(
     n_shot, n_sub, inv_ref, ids_ref, src_ref, cour_hbm, prev_hbm, now_hbm, acc_hbm,
     last, smooth,
-    even, odd, cour, acc, grad, packed, recv, rids, tiles, taps, scale,
-    lsem, asem, hsend, hrecv, isend, irecv, dsend, drecv, nsend, nrecv,
+    even, odd, cour, acc, grad, packed, recv, rids, tiles, taps, scale, along,
+    lsem, hsend, hrecv, isend, irecv, dsend, drecv, nsend, nrecv,
 ):
     buf = (even, odd)
     shot, sub = lax.axis_index("shot"), lax.axis_index("sub")
@@ -94,6 +96,22 @@
     def slab(j):
         return chunk * (rising * j + (1 - rising) * (chunks - 1 - j))
 
+    barrier = pltpu.get_barrier_semaphore()
+
+    def peer_of(m):
+        return lax.rem(shot + m, n_shot)
+
+    for m in range(1, n_shot):
+        pl.semaphore_signal(barrier, inc=1, device_id={"shot": peer_of(m)}, device_id_type=MESH)
+
+    @pl.when(has_front)
+    def _():
+        pl.semaphore_signal(barrier, inc=1, device_id={"sub": front}, device_id_type=MESH)
+
+    @pl.when(has_back)
+    def _():
+        pl.semaphore_signal(barrier, inc=1, device_id={"sub": back}, device_id_type=MESH)
+
     def load(which, j):
         part = pl.ds(slab(j), chunk)
         inside = pl.ds(slab(j) + HALO, chunk)
@@ -101,39 +119,17 @@
             return pltpu.make_async_copy(now_hbm.at[0, part], even.at[inside, inner, :], lsem.at[0, j])
         if which == 1:
             return pltpu.make_async_copy(prev_hbm.at[0, part], odd.at[inside, inner, :], lsem.at[1, j])
-        return pltpu.make_async_copy(cour_hbm.at[0, part], cour.at[part], lsem.at[2, j])
-
-    def load_acc(t, j):
-        part = pl.ds(slab(j), chunk)
-        return pltpu.make_async_copy(acc_hbm.at[0, t, part], acc.at[t, part], asem.at[t, j])
+        if which == 2:
+            return pltpu.make_async_copy(cour_hbm.at[0, part], cour.at[part], lsem.at[2, j])
+        return pltpu.make_async_copy(acc_hbm.at[0, :, part], acc.at[:, part], lsem.at[3, j])
 
     load(0, 0).start()
-    for i in range(chunks + steps - 1):
-        for t in range(steps):
-            j = i - t
-            if 0 <= j < chunks:
-                if t == 0:
-                    if j + 1 < chunks:
-                        load(0, j + 1).start()
-                    load(1, j).start()
-                    load(2, j).start()
-                load_acc(t, j).start()
-
-    barrier = pltpu.get_barrier_semaphore()
-
-    def peer_of(m):
-        return lax.rem(shot + m, n_shot)
-
-    for m in range(1, n_shot):
-        pl.semaphore_signal(barrier, inc=1, device_id={"shot": peer_of(m)}, device_id_type=MESH)
-
-    @pl.when(has_front)
-    def _():
-        pl.semaphore_signal(barrier, inc=1, device_id={"sub": front}, device_id_type=MESH)
-
-    @pl.when(has_back)
-    def _():
-        pl.semaphore_signal(barrier, inc=1, device_id={"sub": back}, device_id_type=MESH)
+    load(0, 1).start()
+    for j in (1, 0, *range(2, chunks)):
+        if 0 < j < chunks - 1:
+            load(0, j + 1).start()
+        for which in (1, 2, 3):
+            load(which, j).start()
 
     for ref in buf:
         for rim in (0, PAD + rows):
@@ -186,48 +182,77 @@
         peer = peer_of(m)
         return pltpu.make_async_remote_copy(
             src_ref=ids_ref.at[pl.ds(CAP * peer, CAP)], dst_ref=rids.at[pl.ds(CAP * m, CAP)],
-            send_sem=isend.at[m], recv_sem=irecv.at[m],
-            device_id={"shot": peer}, device_id_type=MESH,
+            send_sem=isend, recv_sem=irecv, device_id={"shot": peer}, device_id_type=MESH,
         )
 
     def data_copy(j, m):
         peer = peer_of(m)
         return pltpu.make_async_remote_copy(
             src_ref=packed.at[j, pl.ds(CAP * peer, CAP)], dst_ref=recv.at[j, pl.ds(CAP * m, CAP)],
-            send_sem=dsend.at[j, m], recv_sem=drecv.at[j, m],
+            send_sem=dsend.at[j], recv_sem=drecv.at[j],
             device_id={"shot": peer}, device_id_type=MESH,
+        )
+
+    others = pl.ds(CAP, places - CAP)
+
+    def ids_all():
+        return pltpu.make_async_remote_copy(
+            src_ref=ids_ref.at[others], dst_ref=rids.at[others],
+            send_sem=isend, recv_sem=irecv, device_id={"shot": peer_of(1)}, device_id_type=MESH,
+        )
+
+    def data_all(j):
+        return pltpu.make_async_remote_copy(
+            src_ref=packed.at[j, others], dst_ref=recv.at[j, others],
+            send_sem=dsend.at[j], recv_sem=drecv.at[j],
+            device_id={"shot": peer_of(1)}, device_id_type=MESH,
         )
 
     for m in range(1, n_shot):
         ids_copy(m).start()
 
-    lane = lax.broadcasted_iota(jnp.int32, (TX, cols), 1)
-    from_left = [None] + [jnp.where(lane >= d, stencil_weights[d], 0.0) for d in range(1, 5)]
-    from_right = [None] + [jnp.where(lane < cols - d, stencil_weights[d], 0.0) for d in range(1, 5)]
+    across = lax.broadcasted_iota(jnp.int32, (cols, cols), 0) - lax.broadcasted_iota(jnp.int32, (cols, cols), 1)
+    across = jnp.maximum(across, -across)
+    matrix = jnp.where(across == 0, 3.0 * stencil_weights[0], 0.0)
+    for d in range(1, 5):
+        matrix = jnp.where(across == d, stencil_weights[d], matrix)
+    coarse = matrix.astype(jnp.bfloat16)
+    along[0:cols] = coarse
+    along[cols : 2 * cols] = coarse
+    along[2 * cols :] = (matrix - coarse.astype(jnp.float32)).astype(jnp.bfloat16)
 
     def advance(t, j):
         cur, nxt = buf[t % 2], buf[(t + 1) % 2]
         z0 = slab(j)
 
         def block(i, _):
+            column = []
+            for u in range(UNROLL):
+                here = pl.ds(pl.multiple_of((i * UNROLL + u) * TX + PAD, TX), TX)
+                column.append({k: cur[z0 + (k + HALO), here, :] for k in range(-HALO, chunk + HALO)})
+            centre = jnp.concatenate([column[u][k] for u in range(UNROLL) for k in range(chunk)], axis=0)
+            high = centre.astype(jnp.bfloat16)
+            low = (centre - high.astype(jnp.float32)).astype(jnp.bfloat16)
+            lap_y = jnp.dot(
+                jnp.concatenate([high, low, high], axis=1), along[...], preferred_element_type=jnp.float32
+            )
             for u in range(UNROLL):
                 xb = i * UNROLL + u
                 x0 = pl.multiple_of(xb * TX, TX)
                 own = pl.ds(x0, TX)
                 here = pl.ds(pl.multiple_of(x0 + PAD, TX), TX)
-                col = {k: cur[z0 + (k + HALO), here, :] for k in range(-HALO, chunk + HALO)}
+                col = column[u]
                 for k in range(chunk):
                     z = z0 + k
                     c = col[k]
-                    lap = (3.0 * stencil_weights[0]) * c
+                    n = (u * chunk + k) * TX
+                    lap = lap_y[n : n + TX]
                     for d in range(1, 5):
                         pair = (col[k + d] + col[k - d]) + (
                             cur[z + HALO, pl.ds(x0 + (PAD + d), TX), :]
                             + cur[z + HALO, pl.ds(x0 + (PAD - d), TX), :]
                         )
                         lap = lap + stencil_weights[d] * pair
-                        lap = lap + from_left[d] * pltpu.roll(c, d, 1)
-                        lap = lap + from_right[d] * pltpu.roll(c, cols - d, 1)
                     source = src_ref[pl.ds((z * rows + x0) * steps + t, TX, stride=steps), :]
                     adv = (2.0 * c - nxt[z + HALO, here, :]) + (cour[z, own, :] * lap + source)
                     if t + 1 < steps:
@@ -252,49 +277,59 @@
             data_copy(j, m).start()
 
     load(0, 0).wait()
+    load(0, 1).wait()
+
+    def step(t, j):
+        if t == 0:
+            @pl.when((j > 0) & (j < chunks - 1))
+            def _():
+                load(0, j + 1).wait()
+
+            for which in (1, 2, 3):
+                load(which, j).wait()
+
+        @pl.when(j == 0)
+        def _():
+            wait_halo(t, 0)
+
+        @pl.when(j == chunks - 1)
+        def _():
+            wait_halo(t, 1)
+
+        advance(t, j)
+        if t + 1 < steps:
+            @pl.when(j == 0)
+            def _():
+                start_halo(t + 1, 0)
+
+            @pl.when(j == chunks - 1)
+            def _():
+                start_halo(t + 1, 1)
+        else:
+            send(j)
 
     def sweep(i, _):
-        for t in range(steps):
+        many = jnp.where(i == 0, 2, jnp.where(i == 2, 0, jnp.where(i < chunks, 1, 0)))
+
+        def initial(n, _):
+            step(0, jnp.where(i == 0, 1 - n, jnp.where(i == 1, 2, i)))
+            return 0
+
+        lax.fori_loop(0, many, initial, 0)
+        for t in range(1, steps):
             j = i - t
 
             @pl.when((j >= 0) & (j < chunks))
             def _():
-                if t == 0:
-                    @pl.when(j + 1 < chunks)
-                    def _():
-                        load(0, j + 1).wait()
-
-                    load(1, j).wait()
-                    load(2, j).wait()
-                load_acc(t, j).wait()
-
-                @pl.when(j == 0)
-                def _():
-                    wait_halo(t, 0)
-
-                @pl.when(j == chunks - 1)
-                def _():
-                    wait_halo(t, 1)
-
-                advance(t, j)
-                if t + 1 < steps:
-                    @pl.when(j == 0)
-                    def _():
-                        start_halo(t + 1, 0)
-
-                    @pl.when(j == chunks - 1)
-                    def _():
-                        start_halo(t + 1, 1)
-                else:
-                    send(j)
+                step(t, j)
 
         return 0
 
     lax.fori_loop(0, chunks + steps - 1, sweep, 0)
 
-    far = lax.broadcasted_iota(jnp.int32, taps.shape, 0).astype(jnp.float32)
-    ratio = 2.0 * far / depth
-    taps[...] = jnp.exp(-(ratio * ratio))
+    far = lax.broadcasted_iota(jnp.int32, taps.shape, 0) - (2 * depth + chunk)
+    ratio = 2.0 * far.astype(jnp.float32) / depth
+    taps[...] = jnp.where(jnp.maximum(far, -far) <= depth, jnp.exp(-(ratio * ratio)), 0.0)
     row_i = lax.broadcasted_iota(jnp.int32, (depth, 3 * depth), 0)
     row_j = lax.broadcasted_iota(jnp.int32, (depth, 3 * depth), 1) - depth
     gap = row_i - row_j
@@ -307,16 +342,13 @@
 
     def spread(first, low, high):
         def row(i, _):
-            w = []
-            for k in range(chunk):
-                gap = i - (first + k - depth)
-                away = jnp.maximum(gap, -gap)
-                w.append(jnp.where(away <= depth, taps[jnp.minimum(away, depth)], 0.0))
+            gap = i - (first - depth) + (2 * depth + chunk)
+            w = [taps[gap - k] for k in range(chunk)]
             for g in range(TILES_OWN):
-                s = smooth[g, i]
-                for k in range(chunk):
-                    s = s + w[k] * tiles[first + k, g]
-                smooth[g, i] = s
+                s = w[0] * tiles[first, g] + w[1] * tiles[first + 1, g]
+                for k in range(2, chunk, 2):
+                    s = s + (w[k] * tiles[first + k, g] + w[k + 1] * tiles[first + k + 1, g])
+                smooth[g, i] += s
             return 0
 
         lax.fori_loop(low, high, row, 0)
@@ -366,12 +398,10 @@
             pass_on(j, 0).wait_recv()
             spread(2 * depth + z0, z0, depth)
 
-    for m in range(1, n_shot):
-        ids_copy(m).wait()
-
-    def gather(j, _):
-        for m in range(1, n_shot):
-            data_copy(j, m).wait()
+    ids_all().wait()
+
+    def gather(j):
+        data_all(j).wait()
         collect(j)
 
         @pl.when(has_low)
@@ -384,13 +414,18 @@
 
         spread(depth + slab(j), 0, depth)
 
+    def gathers(j, _):
+        gather(j)
+
         @pl.when(j > 0)
         def _():
             finish(j - 1)
 
         return 0
 
-    lax.fori_loop(0, chunks, gather, 0)
+    lax.fori_loop(0, chunks - 1, gathers, 0)
+    finish(chunks - 2)
+    gather(chunks - 1)
     finish(chunks - 1)
 
     def normal(i, _):
@@ -469,16 +504,16 @@
             pltpu.VMEM((chunks, places, HALO, TX, cols), f32),
             pltpu.VMEM((places, TX, cols), jnp.int32),
             pltpu.VMEM((3 * depth, TILES_OWN, TX, cols), f32),
-            pltpu.VMEM((depth + 1, TX, cols), f32),
+            pltpu.VMEM((4 * depth + 2 * HALO, TX, cols), f32),
             pltpu.VMEM((depth, cols), f32),
-            pltpu.SemaphoreType.DMA((3, chunks)),
-            pltpu.SemaphoreType.DMA((steps, chunks)),
+            pltpu.VMEM((3 * cols, cols), jnp.bfloat16),
+            pltpu.SemaphoreType.DMA((4, chunks)),
             pltpu.SemaphoreType.DMA((steps, 2)),
             pltpu.SemaphoreType.DMA((steps, 2)),
-            pltpu.SemaphoreType.DMA((n_shot,)),
-            pltpu.SemaphoreType.DMA((n_shot,)),
-            pltpu.SemaphoreType.DMA((chunks, n_shot)),
-            pltpu.SemaphoreType.DMA((chunks, n_shot)),
+            pltpu.SemaphoreType.DMA,
+            pltpu.SemaphoreType.DMA,
+            pltpu.SemaphoreType.DMA((chunks,)),
+            pltpu.SemaphoreType.DMA((chunks,)),
             pltpu.SemaphoreType.DMA((chunks, 2)),
             pltpu.SemaphoreType.DMA((chunks, 2)),
         ],

time: 77.7 us -> 73 us (0.940); the launches traced: 76.5 us -> 72.8 us
  Pallas kernels: 75.8 us -> 72.2 us
    pallas_call x1, Pallas kernels: 69.5 us -> 65.9 us  [body(): pl.pallas_call(functools.partial(adjoint_kernel, n_shot, n_sub), out_shap...]
where the time goes in v3:
time: 73 us; the launch traced here: 72.8 us
  Pallas kernels  72.2 us (99%)
    pallas_call x1, Pallas kernels, body(): pl.pallas_call(functools.partial(adjoint_kernel, n_shot, n_sub), out_shap...  65.9 us
    pallas_call x1, Pallas kernels, body(): pl.pallas_call(functools.partial(prepare_kernel, depth * rows * cols, col...  4.54 us
    pallas_call x1, Pallas kernels, body(): pl.pallas_call(store_kernel, out_shape=tuple((pltpu.HBM(x.shape, f32) for...  1.68 us

profile of v3, /device:TPU:11, one launch (start us, length us, event | category | flops | bytes accessed | tf_op | source)
XLA Modules:
  0.0 72.8 jit_solution(2293153409438944967)
XLA Ops:
  0.6 4.5 %prepare.1 = (f32[16392,128]{1,0:T(8,128)S(1)}, s32[16]{0:T(128)S(1)}, s32[16,8,128]{2,1,0:T(8,128)S(1)}) custom-call(s32[1,512]{1,0:T(1,128)} %rec_hbm.1, f32[1,4,512]{2,1,0:T(4,128)} %tr_hbm.1, s32[16]{0:T(128)} %bitcast.2, s32[16]{0:T(128)} %bitcast.3), custom_call_target="tpu_custom_call" | custom-call | tf_op jit(solution)/shard_map/prepare/pallas_call | solution.py:468
  5.2 65.9 %adjoint.1 = (f32[1,32,128,128]{3,2,1,0:T(8,128)S(1)}, f32[8,32,8,128]{3,2,1,0:T(8,128)S(1)}) custom-call(s32[16]{0:T(128)S(1)} %get-tuple-element.7.inv_ref, s32[16,8,128]{2,1,0:T(8,128)S(1)} %get-tuple-element.8.ids_ref, f32[16392,128]{1,0:T(8,128)S(1)} %get-tuple-element.9.src_ref, f32[1,32,128,128]{3,2,1,0:T(8,128)} %cour_hbm.1, ...), custom_call_target="tpu_custom_call" | custom-call | tf_op jit(solution)/shard_map/adjoint/pallas_call | solution.py:489
  71.1 1.7 %store.1 = (f32[8,32,8,128]{3,2,1,0:T(8,128)}, f32[1,32,128,128]{3,2,1,0:T(8,128)}) custom-call(f32[8,32,8,128]{3,2,1,0:T(8,128)S(1)} %get-tuple-element.10.smooth_ref, f32[1,32,128,128]{3,2,1,0:T(8,128)S(1)} %get-tuple-element.11.last_ref), custom_call_target="tpu_custom_call" | custom-call | tf_op jit(solution)/shard_map/store/pallas_call | solution.py:529

commit v4 on v3

--- a/solution.py
+++ b/solution.py
@@ -51,13 +51,21 @@
     def add(g, _):
         first = pl.multiple_of(g * group, group)
         values = tr_ref[0, :, pl.ds(first, group)]
-        for r in range(group):
+        def place(r):
             off = rec_ref[0, first + r] - base
             row = jnp.right_shift(off, shift)
             row = jnp.minimum(row.astype(jnp.uint32), jnp.uint32(spare)).astype(jnp.int32)
-            at = pl.ds(pl.multiple_of(row * steps, steps), steps)
             value = jnp.broadcast_to(values[:, r : r + 1], (steps, cols_y))
-            src_ref[at, :] += jnp.where(lane == jnp.bitwise_and(off, cols_y - 1), value, 0.0)
+            value = jnp.where(lane == jnp.bitwise_and(off, cols_y - 1), value, 0.0)
+            return row, pl.ds(pl.multiple_of(row * steps, steps), steps), value
+
+        for r in range(0, group, 2):
+            row_a, at_a, value_a = place(r)
+            row_b, at_b, value_b = place(r + 1)
+            old_a, old_b = src_ref[at_a, :], src_ref[at_b, :]
+            both = jnp.where(row_a == row_b, value_a, 0.0)
+            src_ref[at_a, :] = old_a + value_a
+            src_ref[at_b, :] = old_b + (value_b + both)
         return 0
 
     lax.fori_loop(0, rec_ref.shape[1] // group, add, 0)
@@ -147,6 +155,16 @@
     def _():
         clear(HALO + depth)
 
+    across = lax.broadcasted_iota(jnp.int32, (cols, cols), 0) - lax.broadcasted_iota(jnp.int32, (cols, cols), 1)
+    across = jnp.maximum(across, -across)
+    matrix = jnp.where(across == 0, 3.0 * stencil_weights[0], 0.0)
+    for d in range(1, 5):
+        matrix = jnp.where(across == d, stencil_weights[d], matrix)
+    coarse = matrix.astype(jnp.bfloat16)
+    along[0:cols] = coarse
+    along[cols : 2 * cols] = coarse
+    along[2 * cols :] = (matrix - coarse.astype(jnp.float32)).astype(jnp.bfloat16)
+
     near = jnp.minimum(sub, 1) + jnp.minimum(n_sub - 1 - sub, 1)
     pl.semaphore_wait(barrier, n_shot - 1 + near)
 
@@ -210,16 +228,6 @@
 
     for m in range(1, n_shot):
         ids_copy(m).start()
-
-    across = lax.broadcasted_iota(jnp.int32, (cols, cols), 0) - lax.broadcasted_iota(jnp.int32, (cols, cols), 1)
-    across = jnp.maximum(across, -across)
-    matrix = jnp.where(across == 0, 3.0 * stencil_weights[0], 0.0)
-    for d in range(1, 5):
-        matrix = jnp.where(across == d, stencil_weights[d], matrix)
-    coarse = matrix.astype(jnp.bfloat16)
-    along[0:cols] = coarse
-    along[cols : 2 * cols] = coarse
-    along[2 * cols :] = (matrix - coarse.astype(jnp.float32)).astype(jnp.bfloat16)
 
     def advance(t, j):
         cur, nxt = buf[t % 2], buf[(t + 1) % 2]

time: 73 us -> 72.1 us (0.988)
  Pallas kernels: 72.2 us -> 71.3 us
    pallas_call x1, Pallas kernels: 4.54 us -> 3.54 us  [body(): pl.pallas_call(functools.partial(prepare_kernel, depth * rows * cols, col...]
where the time goes in v4:
time: 72.1 us; the launch traced here: 71.9 us
  Pallas kernels  71.3 us (99%)
    pallas_call x1, Pallas kernels, body(): pl.pallas_call(functools.partial(adjoint_kernel, n_shot, n_sub), out_shap...  66 us
    pallas_call x1, Pallas kernels, body(): pl.pallas_call(functools.partial(prepare_kernel, depth * rows * cols, col...  3.54 us
    pallas_call x1, Pallas kernels, body(): pl.pallas_call(store_kernel, out_shape=tuple((pltpu.HBM(x.shape, f32) for...  1.68 us

profile of v4, /device:TPU:11, one launch (start us, length us, event | category | flops | bytes accessed | tf_op | source)
XLA Modules:
  0.0 71.9 jit_solution(10635994655743906698)
XLA Ops:
  0.6 3.5 %prepare.1 = (f32[16392,128]{1,0:T(8,128)S(1)}, s32[16]{0:T(128)S(1)}, s32[16,8,128]{2,1,0:T(8,128)S(1)}) custom-call(s32[1,512]{1,0:T(1,128)} %rec_hbm.1, f32[1,4,512]{2,1,0:T(4,128)} %tr_hbm.1, s32[16]{0:T(128)} %bitcast.2, s32[16]{0:T(128)} %bitcast.3), custom_call_target="tpu_custom_call" | custom-call | tf_op jit(solution)/shard_map/prepare/pallas_call | solution.py:476
  4.2 66.0 %adjoint.1 = (f32[1,32,128,128]{3,2,1,0:T(8,128)S(1)}, f32[8,32,8,128]{3,2,1,0:T(8,128)S(1)}) custom-call(s32[16]{0:T(128)S(1)} %get-tuple-element.7.inv_ref, s32[16,8,128]{2,1,0:T(8,128)S(1)} %get-tuple-element.8.ids_ref, f32[16392,128]{1,0:T(8,128)S(1)} %get-tuple-element.9.src_ref, f32[1,32,128,128]{3,2,1,0:T(8,128)} %cour_hbm.1, ...), custom_call_target="tpu_custom_call" | custom-call | tf_op jit(solution)/shard_map/adjoint/pallas_call | solution.py:497
  70.2 1.7 %store.1 = (f32[8,32,8,128]{3,2,1,0:T(8,128)}, f32[1,32,128,128]{3,2,1,0:T(8,128)}) custom-call(f32[8,32,8,128]{3,2,1,0:T(8,128)S(1)} %get-tuple-element.10.smooth_ref, f32[1,32,128,128]{3,2,1,0:T(8,128)S(1)} %get-tuple-element.11.last_ref), custom_call_target="tpu_custom_call" | custom-call | tf_op jit(solution)/shard_map/store/pallas_call | solution.py:537
